TPU v7x, 32 devices: a whole 2x2x4 slice. The times are simulated.
32 devices in a mesh: ga: 8 (over z, y), band: 4 (over x, core).
Axes of the slice: x: 2, y: 2, z: 4, core: 2. Of those that a mesh axis runs over, the one named last changes fastest.
Arguments:
- band_coeffs: bfloat16 [8192, 256], P('ga', 'band'), may hold values from -6 to 6
- beta_vectors: bfloat16 [8192, 2048], P('ga'), may hold values from -0.0625 to 0.0625
- atomic_waves: bfloat16 [8192, 1280], P('ga'), may hold values from -0.0625 to 0.0625
- beta_coupling: float32 [2048, 11], replicated, may hold values from -1 to 2
- ortho_inverse: bfloat16 [1280, 1280], replicated, may hold values from -1 to 2
- hubbard_energy: float32 [3], replicated, may hold values from 1 to 4
- band_weight: float32 [256], P('band'), may hold values from 0 to 0.015625
- orbital_start: int32 [1280], replicated, may hold values from 0 to 1277, as said below
- orbital_species: int32 [1280], replicated, may hold values from 0 to 2, as said below
- beta_start: int32 [2048], replicated, may hold values from 0 to 2046, as said below
Outputs:
- hubbard_apply: bfloat16 [8192, 256], P('ga', 'band')
Inputs may be any that keep to these rules, and one draw needn't show every extreme that they name: `orbital_start`: every atom holds 3 or 5 consecutive orbitals; each orbital holds the index of its atom's first orbital. `orbital_species`: orbitals of 5-orbital atoms have species 0 or 1, orbitals of 3-orbital atoms species 2. `beta_start`: every atom holds 2 or 6 consecutive projectors; each projector holds the index of its atom's first projector.
All inputs are finite; a program needn't handle non-finite values.
Results may differ from a plain program's by a relative error of at most 0.0085.
Values sent between devices are 32-bit elements; how exact they have to be, the bound alone decides.
No kernel may reach another device: no remote copies, remote signals or barrier semaphores. Data moves between devices by JAX's collectives and lax.ppermute only.
A program may use at most 64 MiB of HBM per device.

v0:
```python
import jax
import jax.numpy as jnp
from jax import lax
from jax.sharding import PartitionSpec as P

ORB_REACH = 4
BETA_REACH = 5
NSPEC = 3


def rim_shift(extended, reach, offset, rows):
    return lax.slice_in_dim(extended, reach + offset, reach + offset + rows, axis=0)


def same_atom(start_ext, reach, rows):
    centre = rim_shift(start_ext, reach, 0, rows)
    return jnp.stack(
        [
            (rim_shift(start_ext, reach, offset, rows) == centre).astype(jnp.float32)
            for offset in range(-reach, reach + 1)
        ]
    )


def band_apply(coupling, extended, reach, rows):
    total = jnp.zeros((rows, extended.shape[1]), jnp.float32)
    for offset in range(-reach, reach + 1):
        total = total + coupling[offset + reach][:, None] * rim_shift(extended, reach, offset, rows)
    return total


def beta_matrix(beta_coupling, beta_start):
    rows = beta_start.shape[0]
    start_ext = jnp.pad(beta_start, BETA_REACH, constant_values=-1)
    mask = same_atom(start_ext, BETA_REACH, rows)
    padded = jnp.pad(beta_coupling, ((BETA_REACH, BETA_REACH), (0, 0)))
    terms = []
    for offset in range(-BETA_REACH, BETA_REACH + 1):
        mirror = rim_shift(padded, BETA_REACH, offset, rows)[:, BETA_REACH - offset]
        terms.append(0.5 * (beta_coupling[:, BETA_REACH + offset] + mirror))
    return jnp.stack(terms) * mask


def occupancy(extended, weights, mask, reach, rows):
    centre = rim_shift(extended, reach, 0, rows)
    weighted = centre * weights[None, :]
    return (
        jnp.stack(
            [
                jnp.sum(weighted * rim_shift(extended, reach, offset, rows), axis=1)
                for offset in range(-reach, reach + 1)
            ]
        )
        * mask
    )


def hubbard_mix(occupied, u_rows, mask, extended, reach, rows):
    centre_flag = (jnp.arange(2 * reach + 1) == reach).astype(jnp.float32)[:, None]
    potential = u_rows[None, :] * (0.5 * centre_flag - occupied) * mask
    return band_apply(potential, extended, reach, rows)


def per_orbital_u(species, hubbard_energy):
    onehot = (species[:, None] == jnp.arange(NSPEC)[None, :]).astype(jnp.float32)
    return jnp.dot(onehot, hubbard_energy, precision=lax.Precision.HIGHEST)


def shards(
    band_coeffs,
    beta_vectors,
    atomic_waves,
    beta_coupling,
    ortho_inverse,
    hubbard_energy,
    band_weight,
    orbital_start,
    orbital_species,
    beta_start,
):
    highest = lax.Precision.HIGHEST
    nbeta = beta_vectors.shape[1]
    norbit = atomic_waves.shape[1]
    coupling = beta_matrix(beta_coupling, beta_start)
    beta_correlation = lax.psum(
        jnp.dot(beta_vectors.T, band_coeffs, preferred_element_type=jnp.float32), "ga"
    )
    corrected = band_apply(
        coupling, jnp.pad(beta_correlation, ((BETA_REACH, BETA_REACH), (0, 0))), BETA_REACH, nbeta
    ).astype(jnp.bfloat16)
    correlation_psi = (
        band_coeffs.astype(jnp.float32)
        + jnp.dot(beta_vectors, corrected, preferred_element_type=jnp.float32)
    ).astype(jnp.bfloat16)
    partial_value = jnp.dot(atomic_waves.T, correlation_psi, preferred_element_type=jnp.float32)
    u_full = per_orbital_u(orbital_species, hubbard_energy)
    start_full = jnp.pad(orbital_start, ORB_REACH, constant_values=-1)
    ortho_full = ortho_inverse.astype(jnp.float32)
    summed = lax.psum(partial_value, "ga")
    projections = jnp.dot(ortho_full, summed, precision=highest)
    extended = jnp.pad(projections, ((ORB_REACH, ORB_REACH), (0, 0)))
    mask = same_atom(start_full, ORB_REACH, norbit)
    occupied = lax.psum(occupancy(extended, band_weight, mask, ORB_REACH, norbit), "band")
    mixed = hubbard_mix(occupied, u_full, mask, extended, ORB_REACH, norbit)
    rotated = jnp.dot(ortho_full, mixed, precision=highest)
    rotated_half = rotated.astype(jnp.bfloat16)
    hubbard_waves = jnp.dot(atomic_waves, rotated_half, preferred_element_type=jnp.float32)
    wave_half = hubbard_waves.astype(jnp.bfloat16)
    beta_update = lax.psum(
        jnp.dot(beta_vectors.T, wave_half, preferred_element_type=jnp.float32), "ga"
    )
    correction = band_apply(
        coupling, jnp.pad(beta_update, ((BETA_REACH, BETA_REACH), (0, 0))), BETA_REACH, nbeta
    ).astype(jnp.bfloat16)
    return (
        hubbard_waves + jnp.dot(beta_vectors, correction, preferred_element_type=jnp.float32)
    ).astype(jnp.bfloat16)


def solution(mesh):
    placed = (
        P("ga", "band"),
        P("ga", None),
        P("ga", None),
        P(),
        P(),
        P(),
        P("band"),
        P(),
        P(),
        P(),
    )
    return jax.shard_map(
        shards, mesh=mesh, in_specs=placed, out_specs=P("ga", "band"), check_vma=False
    )
```

profile of v0, /device:TPU:0, one launch (start us, length us, event | category | flops | bytes accessed | tf_op | source)
XLA Modules:
  0.0 279.5 jit_solution(14939464274968887758)
XLA Ops:
  6.5 4.1 %fusion.134 = f32[2048,64]{0,1:T(8,128)} fusion(bf16[1024,64]{0,1:T(8,128)(2,1)} %param.10, bf16[1024,2048]{1,0:T(8,128)(2,1)} %param.11), kind=kOutput, calls=%fused_computation.207 | convolution fusion | flops 268435456 | bytes 4849664 | tf_op jit(solution)/shard_map/dot_general | solution.py:86
  10.6 0.0 all-reduce.10.cloned.1.call-update
  10.6 0.0 all-reduce.12.cloned.1.call-start
  10.7 0.1 multiply_bitcast_fusion.8
  10.8 0.9 multiply_bitcast_fusion
  11.6 0.1 fusion.117
  11.7 0.2 stack.181
  11.9 1.7 stack.160
  13.6 0.1 fusion.132
  13.7 72.5 %all-reduce.10.cloned.1.call-done = f32[2048,64]{0,1:T(8,128)} async-done(((f32[2048,64]{0,1:T(8,128)}), f32[2048,64]{0,1:T(8,128)}) %all-reduce.10.cloned.1.call-update) | async-done | bytes 524304 | tf_op jit(solution)/shard_map/psum | solution.py:85
  86.2 8.8 %convolution_bitcast_fusion.2 = f32[1280,64]{0,1:T(8,128)} fusion(bf16[1024,1280]{1,0:T(8,128)(2,1)} %param.12, bf16[1024,2048]{1,0:T(8,128)(2,1)} %param.11, f32[2048,64]{0,1:T(8,128)} %all-reduce.10.cloned.1.call-done, f32[2048]{0:T(1024)S(1)} %bitcast.85, f32[2048]{0:T(1024)S(1)} %bitcast.87, f32[2048]{0:T(1024)S(1)} %bitcast.89, f32[2048]{0:T(1024)S(1)} %bitcast.91, ...), kind=kOutput, calls=%fused_computation.2 | convolution fusion | flops 439287808 | bytes 7888896 | tf_op jit(solution)/shard_map/dot_general | solution.py:95
  95.1 0.0 copy-start.15
  95.1 0.0 all-reduce.12.cloned.1.call-update
  95.1 0.0 all-reduce.14.cloned.1.call-start
  95.2 0.1 fusion.116
  95.4 0.1 stack.208
  95.5 0.5 convolution_reduce_fusion
  96.1 69.8 %all-reduce.12.cloned.1.call-done = f32[1280,64]{0,1:T(8,128)} async-done(((f32[1280,64]{0,1:T(8,128)}), f32[1280,64]{0,1:T(8,128)}) %all-reduce.12.cloned.1.call-update) | async-done | bytes 327696 | tf_op jit(solution)/shard_map/psum | solution.py:99
  165.9 4.0 %convolution_bitcast_fusion.1 = f32[1280,64]{0,1:T(8,128)S(1)} fusion(f32[1280,64]{0,1:T(8,128)} %all-reduce.12.cloned.1.call-done, bf16[1280,1280]{1,0:T(8,128)(2,1)S(1)} %copy-done), kind=kOutput, calls=%fused_computation.1 | convolution fusion | flops 1258291200 | bytes 3932160 | tf_op jit(solution)/shard_map/dot_general | solution.py:100
  169.9 0.7 copy-done.2
  170.6 0.8 fusion.26
  171.5 0.1 stack.191
  171.6 11.1 %psum.30 = f32[9,1280]{1,0:T(8,128)S(1)} all-reduce(f32[9,1280]{1,0:T(8,128)S(1)} %mul.535), channel_id=1, replica_groups=mesh['ga'=8,'band'=4] {'band'}, use_global_device_ids=true, to_apply=%region_11.12 | all-reduce | flops 11520 | bytes 92160 | tf_op jit(solution)/shard_map/psum | solution.py:103
  182.7 0.0 copy-start.1
  182.7 0.1 multiply_multiply_fusion.9
  182.8 0.1 slice_reduce_fusion.8
  183.0 5.8 %convolution_convert_fusion = bf16[64,1280]{1,0:T(8,128)(2,1)S(1)} fusion(bf16[1280,1280]{1,0:T(8,128)(2,1)S(1)} %copy-done, f32[1280,64]{0,1:T(8,128)} %copy-done.2, f32[1280]{0:T(1024)S(1)} %get-tuple-element.15, f32[1280]{0:T(1024)S(1)} %get-tuple-element.16, f32[1280]{0:T(1024)S(1)} %get-tuple-element.17, f32[1280]{0:T(1024)S(1)} %get-tuple-element.18, ...), kind=kOutput, calls=%fused_computation.3 | convolution fusion | flops 1259765760 | bytes 3814400 | tf_op jit(solution)/shard_map/dot_general | solution.py:105
  188.7 2.6 fusion.133
  191.4 1.7 convolution_bitcast_fusion
  193.1 0.0 all-reduce.14.cloned.1.call-update
  193.1 72.4 %all-reduce.14.cloned.1.call-done = f32[2048,64]{0,1:T(8,128)} async-done(((f32[2048,64]{0,1:T(8,128)}), f32[2048,64]{0,1:T(8,128)}) %all-reduce.14.cloned.1.call-update) | async-done | bytes 524304 | tf_op jit(solution)/shard_map/psum | solution.py:109
  265.5 7.5 %fusion.3 = bf16[1024,64]{0,1:T(8,128)(2,1)} fusion(f32[64,1024]{1,0:T(8,128)S(1)} %fusion.133, bf16[1024,2048]{1,0:T(8,128)(2,1)} %param.11, f32[2048,64]{0,1:T(8,128)} %all-reduce.14.cloned.1.call-done, f32[2048]{0:T(1024)S(1)} %bitcast.86, f32[2048]{0:T(1024)} %bitcast.88, f32[2048]{0:T(1024)} %bitcast.90, f32[2048]{0:T(1024)} %bitcast.92, ...), kind=kOutput, calls=%fused_computation.9 | convolution fusion | flops 271450112 | bytes 5201920 | tf_op jit(solution)/shard_map/dot_general | solution.py:116
  (56 shorter events, 0.2 us)
Async XLA Ops:
  6.5 159.3 %copy-start = (bf16[1280,1280]{1,0:T(8,128)(2,1)S(1)}, bf16[1280,1280]{1,0:T(8,128)(2,1)}, u32[]{:S(2)}) copy-start(bf16[1280,1280]{1,0:T(8,128)(2,1)} %param.14) | copy-start | bytes 9830404
  6.5 4.1 %copy-start.3 = (f32[2048,11]{0,1:T(8,128)S(1)}, f32[2048,11]{0,1:T(8,128)}, u32[]{:S(2)}) copy-start(f32[2048,11]{0,1:T(8,128)} %param.13) | copy-start | bytes 270340
  6.5 5.1 %copy-start.14 = (s32[2048]{0:T(1024)S(1)}, s32[2048]{0:T(1024)}, u32[]{:S(2)}) copy-start(s32[2048]{0:T(1024)} %param.19) | copy-start | bytes 24580
  6.5 79.7 %all-reduce.10.cloned.1.call-start = ((), (), s32[]{:S(2)}) async-start(), calls=%async_computation | async-start | bytes 1048576 | tf_op jit(solution)/shard_map/psum | solution.py:85
  10.6 155.2 %all-reduce.12.cloned.1.call-start = ((), (), s32[]{:S(2)}) async-start(), calls=%async_computation.1 | async-start | bytes 655360 | tf_op jit(solution)/shard_map/psum | solution.py:99
  13.7 81.4 %copy-start.5 = (f32[1,2048]{1,0:T(1,128)}, f32[1,2048]{1,0:T(1,128)S(1)}, u32[]{:S(2)}) copy-start(f32[1,2048]{1,0:T(1,128)S(1)} %get-tuple-element.25) | copy-start | bytes 24580
  13.7 81.4 %copy-start.6 = (f32[1,2048]{1,0:T(1,128)}, f32[1,2048]{1,0:T(1,128)S(1)}, u32[]{:S(2)}) copy-start(f32[1,2048]{1,0:T(1,128)S(1)} %get-tuple-element.26) | copy-start | bytes 24580
  13.7 81.3 %copy-start.7 = (f32[1,2048]{1,0:T(1,128)}, f32[1,2048]{1,0:T(1,128)S(1)}, u32[]{:S(2)}) copy-start(f32[1,2048]{1,0:T(1,128)S(1)} %get-tuple-element.27) | copy-start | bytes 24580
  13.7 81.3 %copy-start.8 = (f32[1,2048]{1,0:T(1,128)}, f32[1,2048]{1,0:T(1,128)S(1)}, u32[]{:S(2)}) copy-start(f32[1,2048]{1,0:T(1,128)S(1)} %get-tuple-element.28) | copy-start | bytes 24580
  13.7 81.3 %copy-start.9 = (f32[1,2048]{1,0:T(1,128)}, f32[1,2048]{1,0:T(1,128)S(1)}, u32[]{:S(2)}) copy-start(f32[1,2048]{1,0:T(1,128)S(1)} %get-tuple-element.29) | copy-start | bytes 24580
  13.7 81.3 %copy-start.10 = (f32[1,2048]{1,0:T(1,128)}, f32[1,2048]{1,0:T(1,128)S(1)}, u32[]{:S(2)}) copy-start(f32[1,2048]{1,0:T(1,128)S(1)} %get-tuple-element.30) | copy-start | bytes 24580
  13.7 81.3 %copy-start.11 = (f32[1,2048]{1,0:T(1,128)}, f32[1,2048]{1,0:T(1,128)S(1)}, u32[]{:S(2)}) copy-start(f32[1,2048]{1,0:T(1,128)S(1)} %get-tuple-element.31) | copy-start | bytes 24580
  13.7 81.3 %copy-start.12 = (f32[1,2048]{1,0:T(1,128)}, f32[1,2048]{1,0:T(1,128)S(1)}, u32[]{:S(2)}) copy-start(f32[1,2048]{1,0:T(1,128)S(1)} %get-tuple-element.32) | copy-start | bytes 24580
  13.7 81.3 %copy-start.13 = (f32[1,2048]{1,0:T(1,128)}, f32[1,2048]{1,0:T(1,128)S(1)}, u32[]{:S(2)}) copy-start(f32[1,2048]{1,0:T(1,128)S(1)} %get-tuple-element.33) | copy-start | bytes 24580
  86.2 8.9 %copy-start.4 = (s32[1280]{0:T(1024)S(1)}, s32[1280]{0:T(1024)}, u32[]{:S(2)}) copy-start(s32[1280]{0:T(1024)} %param.17) | copy-start | bytes 15364
  86.2 9.3 %copy-start.16 = (s32[1280]{0:T(1024)S(1)}, s32[1280]{0:T(1024)}, u32[]{:S(2)}) copy-start(s32[1280]{0:T(1024)} %param.18) | copy-start | bytes 15364
  86.2 9.3 %copy-start.17 = (f32[3]{0:T(128)S(1)}, f32[3]{0:T(128)}, u32[]{:S(2)}) copy-start(f32[3]{0:T(128)} %param.15) | copy-start | bytes 40
  95.1 75.5 %copy-start.15 = (f32[64]{0:T(128)S(1)}, f32[64]{0:T(128)}, u32[]{:S(2)}) copy-start(f32[64]{0:T(128)} %param.16) | copy-start | bytes 772
  95.1 170.4 %all-reduce.14.cloned.1.call-start = ((), (), s32[]{:S(2)}) async-start(), calls=%async_computation.2 | async-start | bytes 1048576 | tf_op jit(solution)/shard_map/psum | solution.py:109
  169.9 0.7 copy-start.2
  182.7 8.7 %copy-start.1 = (bf16[1024,2048]{1,0:T(8,128)(2,1)S(1)}, bf16[1024,2048]{1,0:T(8,128)(2,1)}, u32[]{:S(2)}) copy-start(bf16[1024,2048]{1,0:T(8,128)(2,1)} %param.11) | copy-start | bytes 12582916
Sparse Core Ops, SparseCore 0:
  10.8 75.4 all-reduce.9
  95.2 70.5 all-reduce.11
  193.2 72.2 all-reduce.13
where the time goes:
time: 280 us; the launch traced here: 279 us
  waiting for transfers between devices  215 us (77%)
  matrix products  35 us (12%)
  between operations  13.6 us (5%)
  blocking collectives  11.1 us (4%)
  local copies, waits for them, and re-layouts  3.06 us (1%)
    psum x1, waiting for transfers between devices, shards(): lax.psum(jnp.dot(beta_vectors.T, band_coeffs, preferred_element_type=jnp....  72.5 us
    psum x1, waiting for transfers between devices, shards(): lax.psum(jnp.dot(beta_vectors.T, wave_half, preferred_element_type=jnp.fl...  72.4 us
    psum x1, waiting for transfers between devices, shards(): summed = lax.psum(partial_value, 'ga')  69.8 us
    psum x1, blocking collectives, shards(): lax.psum(occupancy(extended, band_weight, mask, ORB_REACH, norbit), 'band')  11.1 us
    dot_general x1, matrix products, shards(): jnp.dot(atomic_waves.T, correlation_psi, preferred_element_type=jnp.float32)  8.77 us
    dot_general x1, matrix products, shards(): jnp.dot(beta_vectors, correction, preferred_element_type=jnp.float32)  7.46 us
    dot_general x1, matrix products, shards(): rotated = jnp.dot(ortho_full, mixed, precision=highest)  5.79 us
  transfers between devices with their start and end apart: 3, of which 3 were waited for; matrix products, arithmetic and copies ran while one was open for 1% of the time, Pallas kernels for 0%

commit v1 on v0

--- a/solution.py
+++ b/solution.py
@@ -82,8 +82,11 @@
     nbeta = beta_vectors.shape[1]
     norbit = atomic_waves.shape[1]
     coupling = beta_matrix(beta_coupling, beta_start)
-    beta_correlation = lax.psum(
-        jnp.dot(beta_vectors.T, band_coeffs, preferred_element_type=jnp.float32), "ga"
+    beta_correlation = jnp.sum(
+        lax.all_gather(
+            jnp.dot(beta_vectors.T, band_coeffs, preferred_element_type=jnp.float32), "ga"
+        ),
+        axis=0,
     )
     corrected = band_apply(
         coupling, jnp.pad(beta_correlation, ((BETA_REACH, BETA_REACH), (0, 0))), BETA_REACH, nbeta

time: 280 us -> 285 us (1.018)
  local copies, waits for them, and re-layouts: 3.06 us -> 7.63 us
    all_gather x0 -> x1, waiting for transfers between devices: none -> 72.5 us  [shards(): lax.all_gather(jnp.dot(beta_vectors.T, band_coeffs, preferred_element_typ...]
    psum x1 -> x0, waiting for transfers between devices: 72.5 us -> none  [shards(): lax.psum(jnp.dot(beta_vectors.T, band_coeffs, preferred_element_type=jnp....]
    unnamed x36 -> x39, local copies, waits for them, and re-layouts: 0.78 us -> 5.35 us
where the time goes in v1:
time: 285 us
  waiting for transfers between devices  214 us (75%)
  matrix products  34.8 us (12%)
  between operations  13.6 us (5%)
  blocking collectives  11.1 us (4%)
  local copies, waits for them, and re-layouts  7.63 us (3%)
  other arithmetic  3.78 us (1%)
    all_gather x1, waiting for transfers between devices, shards(): lax.all_gather(jnp.dot(beta_vectors.T, band_coeffs, preferred_element_typ...  72.5 us
    psum x1, waiting for transfers between devices, shards(): lax.psum(jnp.dot(beta_vectors.T, wave_half, preferred_element_type=jnp.fl...  72.4 us
    psum x1, waiting for transfers between devices, shards(): summed = lax.psum(partial_value, 'ga')  69.2 us
    psum x1, blocking collectives, shards(): lax.psum(occupancy(extended, band_weight, mask, ORB_REACH, norbit), 'band')  11.1 us
    dot_general x1, matrix products, shards(): jnp.dot(atomic_waves.T, correlation_psi, preferred_element_type=jnp.float32)  8.63 us
    dot_general x1, matrix products, shards(): jnp.dot(beta_vectors, correction, preferred_element_type=jnp.float32)  7.41 us
    dot_general x1, matrix products, shards(): rotated = jnp.dot(ortho_full, mixed, precision=highest)  5.79 us
  transfers between devices with their start and end apart: 3, of which 3 were waited for; matrix products, arithmetic and copies ran while one was open for 1% of the time, Pallas kernels for 0%

profile of v1, /device:TPU:0, one launch (start us, length us, event | category | flops | bytes accessed | tf_op | source)
XLA Modules:
  0.0 285.1 jit_solution(8973181449006062445)
XLA Ops:
  6.5 4.0 %fusion.134 = f32[2048,64]{0,1:T(8,128)} fusion(bf16[1024,64]{0,1:T(8,128)(2,1)} %param.10, bf16[1024,2048]{1,0:T(8,128)(2,1)} %param.11), kind=kOutput, calls=%fused_computation.208 | convolution fusion | flops 268435456 | bytes 4849664 | tf_op jit(solution)/shard_map/dot_general | solution.py:87
  10.6 0.0 all-gather.3.cloned.1.call-update
  10.6 0.0 all-reduce.9.cloned.1.call-start
  10.7 0.1 multiply_bitcast_fusion.8
  10.8 0.2 multiply_bitcast_fusion
  11.0 0.2 stack.160
  11.2 0.7 fusion.117
  11.9 1.7 stack.181
  13.6 0.1 fusion.132
  13.7 72.5 %all-gather.3.cloned.1.call-done = f32[16384,64]{0,1:T(8,128)} async-done(((f32[2048,64]{0,1:T(8,128)}), f32[16384,64]{0,1:T(8,128)}) %all-gather.3.cloned.1.call-update) | async-done | bytes 4194320 | tf_op jit(solution)/shard_map/all_gather | solution.py:86
  86.3 4.6 %copy.11 = f32[8,8,8,2048]{3,2,1,0:T(8,128)S(1)} copy(f32[8,8,8,2048]{3,1,2,0:T(8,128)} %bitcast.78) | data formatting | bytes 8388608
  90.8 1.8 bitcast_reduce_fusion
  92.7 8.6 %convolution_bitcast_fusion.2 = f32[1280,64]{0,1:T(8,128)} fusion(bf16[1024,1280]{1,0:T(8,128)(2,1)} %param.12, bf16[1024,2048]{1,0:T(8,128)(2,1)} %param.11, f32[2048,64]{0,1:T(8,128)} %bitcast_reduce_fusion, f32[2048]{0:T(1024)S(1)} %bitcast.91, f32[2048]{0:T(1024)S(1)} %bitcast.93, f32[2048]{0:T(1024)S(1)} %bitcast.95, f32[2048]{0:T(1024)S(1)} %bitcast.97, ...), kind=kOutput, calls=%fused_computation.3 | convolution fusion | flops 439287808 | bytes 7888896 | tf_op jit(solution)/shard_map/dot_general | solution.py:98
  101.4 0.0 all-reduce.9.cloned.1.call-update
  101.4 0.0 all-reduce.11.cloned.1.call-start
  101.4 0.1 fusion.116
  101.7 0.1 stack.208
  101.8 0.5 convolution_reduce_fusion
  102.3 69.2 %all-reduce.9.cloned.1.call-done = f32[1280,64]{0,1:T(8,128)} async-done(((f32[1280,64]{0,1:T(8,128)}), f32[1280,64]{0,1:T(8,128)}) %all-reduce.9.cloned.1.call-update) | async-done | bytes 327696 | tf_op jit(solution)/shard_map/psum | solution.py:102
  171.5 4.0 %convolution_bitcast_fusion.1 = f32[1280,64]{0,1:T(8,128)S(1)} fusion(f32[1280,64]{0,1:T(8,128)} %all-reduce.9.cloned.1.call-done, bf16[1280,1280]{1,0:T(8,128)(2,1)S(1)} %copy-done), kind=kOutput, calls=%fused_computation.2 | convolution fusion | flops 1258291200 | bytes 3932160 | tf_op jit(solution)/shard_map/dot_general | solution.py:103
  175.6 0.7 copy-done.2
  176.3 0.8 fusion.26
  177.2 0.1 stack.191
  177.3 11.1 %psum.22 = f32[9,1280]{1,0:T(8,128)S(1)} all-reduce(f32[9,1280]{1,0:T(8,128)S(1)} %mul.535), channel_id=1, replica_groups=mesh['ga'=8,'band'=4] {'band'}, use_global_device_ids=true, to_apply=%region_11.12 | all-reduce | flops 11520 | bytes 92160 | tf_op jit(solution)/shard_map/psum | solution.py:106
  188.4 0.1 multiply_multiply_fusion.9
  188.5 0.1 slice_reduce_fusion.8
  188.6 5.8 %convolution_convert_fusion = bf16[64,1280]{1,0:T(8,128)(2,1)S(1)} fusion(bf16[1280,1280]{1,0:T(8,128)(2,1)S(1)} %copy-done, f32[1280,64]{0,1:T(8,128)} %copy-done.2, f32[1280]{0:T(1024)S(1)} %get-tuple-element.15, f32[1280]{0:T(1024)S(1)} %get-tuple-element.16, f32[1280]{0:T(1024)S(1)} %get-tuple-element.17, f32[1280]{0:T(1024)S(1)} %get-tuple-element.18, ...), kind=kOutput, calls=%fused_computation.4 | convolution fusion | flops 1259765760 | bytes 3814400 | tf_op jit(solution)/shard_map/dot_general | solution.py:108
  194.4 2.6 fusion.133
  197.0 1.7 convolution_bitcast_fusion
  198.7 0.0 all-reduce.11.cloned.1.call-update
  198.7 72.4 %all-reduce.11.cloned.1.call-done = f32[2048,64]{0,1:T(8,128)} async-done(((f32[2048,64]{0,1:T(8,128)}), f32[2048,64]{0,1:T(8,128)}) %all-reduce.11.cloned.1.call-update) | async-done | bytes 524304 | tf_op jit(solution)/shard_map/psum | solution.py:112
  271.1 7.4 %fusion.3 = bf16[1024,64]{0,1:T(8,128)(2,1)} fusion(f32[64,1024]{1,0:T(8,128)S(1)} %fusion.133, bf16[1024,2048]{1,0:T(8,128)(2,1)} %param.11, f32[2048,64]{0,1:T(8,128)} %all-reduce.11.cloned.1.call-done, f32[2048]{0:T(1024)S(1)} %bitcast.92, f32[2048]{0:T(1024)} %bitcast.94, f32[2048]{0:T(1024)} %bitcast.96, f32[2048]{0:T(1024)} %bitcast.98, ...), kind=kOutput, calls=%fused_computation.10 | convolution fusion | flops 271450112 | bytes 5201920 | tf_op jit(solution)/shard_map/dot_general | solution.py:119
  (60 shorter events, 0.2 us)
Async XLA Ops:
  6.5 165.0 %copy-start = (bf16[1280,1280]{1,0:T(8,128)(2,1)S(1)}, bf16[1280,1280]{1,0:T(8,128)(2,1)}, u32[]{:S(2)}) copy-start(bf16[1280,1280]{1,0:T(8,128)(2,1)} %param.14) | copy-start | bytes 9830404
  6.5 4.1 %copy-start.3 = (f32[2048,11]{0,1:T(8,128)S(1)}, f32[2048,11]{0,1:T(8,128)}, u32[]{:S(2)}) copy-start(f32[2048,11]{0,1:T(8,128)} %param.13) | copy-start | bytes 270340
  6.5 4.6 %copy-start.15 = (s32[2048]{0:T(1024)S(1)}, s32[2048]{0:T(1024)}, u32[]{:S(2)}) copy-start(s32[2048]{0:T(1024)} %param.19) | copy-start | bytes 24580
  6.5 79.7 %all-gather.3.cloned.1.call-start = ((), (), s32[]{:S(2)}) async-start(), calls=%async_computation.2 | async-start | bytes 4718592 | tf_op jit(solution)/shard_map/all_gather | solution.py:86
  10.6 160.9 %all-reduce.9.cloned.1.call-start = ((), (), s32[]{:S(2)}) async-start(), calls=%async_computation | async-start | bytes 655360 | tf_op jit(solution)/shard_map/psum | solution.py:102
  13.6 79.0 %copy-start.6 = (f32[1,2048]{1,0:T(1,128)}, f32[1,2048]{1,0:T(1,128)S(1)}, u32[]{:S(2)}) copy-start(f32[1,2048]{1,0:T(1,128)S(1)} %get-tuple-element.25) | copy-start | bytes 24580
  13.6 79.0 %copy-start.7 = (f32[1,2048]{1,0:T(1,128)}, f32[1,2048]{1,0:T(1,128)S(1)}, u32[]{:S(2)}) copy-start(f32[1,2048]{1,0:T(1,128)S(1)} %get-tuple-element.26) | copy-start | bytes 24580
  13.7 79.0 %copy-start.8 = (f32[1,2048]{1,0:T(1,128)}, f32[1,2048]{1,0:T(1,128)S(1)}, u32[]{:S(2)}) copy-start(f32[1,2048]{1,0:T(1,128)S(1)} %get-tuple-element.27) | copy-start | bytes 24580
  13.7 79.0 %copy-start.9 = (f32[1,2048]{1,0:T(1,128)}, f32[1,2048]{1,0:T(1,128)S(1)}, u32[]{:S(2)}) copy-start(f32[1,2048]{1,0:T(1,128)S(1)} %get-tuple-element.28) | copy-start | bytes 24580
  13.7 79.0 %copy-start.10 = (f32[1,2048]{1,0:T(1,128)}, f32[1,2048]{1,0:T(1,128)S(1)}, u32[]{:S(2)}) copy-start(f32[1,2048]{1,0:T(1,128)S(1)} %get-tuple-element.29) | copy-start | bytes 24580
  13.7 79.0 %copy-start.11 = (f32[1,2048]{1,0:T(1,128)}, f32[1,2048]{1,0:T(1,128)S(1)}, u32[]{:S(2)}) copy-start(f32[1,2048]{1,0:T(1,128)S(1)} %get-tuple-element.30) | copy-start | bytes 24580
  13.7 79.0 %copy-start.12 = (f32[1,2048]{1,0:T(1,128)}, f32[1,2048]{1,0:T(1,128)S(1)}, u32[]{:S(2)}) copy-start(f32[1,2048]{1,0:T(1,128)S(1)} %get-tuple-element.31) | copy-start | bytes 24580
  13.7 79.0 %copy-start.13 = (f32[1,2048]{1,0:T(1,128)}, f32[1,2048]{1,0:T(1,128)S(1)}, u32[]{:S(2)}) copy-start(f32[1,2048]{1,0:T(1,128)S(1)} %get-tuple-element.32) | copy-start | bytes 24580
  13.7 79.0 %copy-start.14 = (f32[1,2048]{1,0:T(1,128)}, f32[1,2048]{1,0:T(1,128)S(1)}, u32[]{:S(2)}) copy-start(f32[1,2048]{1,0:T(1,128)S(1)} %get-tuple-element.33) | copy-start | bytes 24580
  90.8 1.9 copy-start.4
  92.7 8.7 %copy-start.5 = (s32[1280]{0:T(1024)S(1)}, s32[1280]{0:T(1024)}, u32[]{:S(2)}) copy-start(s32[1280]{0:T(1024)} %param.17) | copy-start | bytes 15364
  92.7 9.0 %copy-start.17 = (s32[1280]{0:T(1024)S(1)}, s32[1280]{0:T(1024)}, u32[]{:S(2)}) copy-start(s32[1280]{0:T(1024)} %param.18) | copy-start | bytes 15364
  92.7 9.0 %copy-start.18 = (f32[3]{0:T(128)S(1)}, f32[3]{0:T(128)}, u32[]{:S(2)}) copy-start(f32[3]{0:T(128)} %param.15) | copy-start | bytes 40
  101.4 74.9 %copy-start.16 = (f32[64]{0:T(128)S(1)}, f32[64]{0:T(128)}, u32[]{:S(2)}) copy-start(f32[64]{0:T(128)} %param.16) | copy-start | bytes 772
  101.4 169.7 %all-reduce.11.cloned.1.call-start = ((), (), s32[]{:S(2)}) async-start(), calls=%async_computation.1 | async-start | bytes 1048576 | tf_op jit(solution)/shard_map/psum | solution.py:112
  175.5 0.7 copy-start.2
  188.4 8.7 %copy-start.1 = (bf16[1024,2048]{1,0:T(8,128)(2,1)S(1)}, bf16[1024,2048]{1,0:T(8,128)(2,1)}, u32[]{:S(2)}) copy-start(bf16[1024,2048]{1,0:T(8,128)(2,1)} %param.11) | copy-start | bytes 12582916
Sparse Core Ops, SparseCore 0:
  10.7 75.4 all-gather.2
  101.5 69.9 all-reduce.8
  198.8 72.2 all-reduce.10
